TPU v7x, 512 devices: a whole 4x8x8 slice. The times are simulated.
512 devices in a mesh: dp: 16 (over x, y_lo), expert: 16 (over z, y_hi), tensor: 2 (over core).
Axes of the slice: x: 4, y: 8 (y_hi: 2, y_lo: 4; y = y_hi * 4 + y_lo), z: 8, core: 2. Of those that a mesh axis runs over, the one named last changes fastest.
Arguments:
- tokens: bfloat16 [32768, 2048], P(('dp', 'expert'), 'tensor'), may hold values from -24 to 24
- routes: int32 [32768, 4], P(('dp', 'expert')), may hold values from 0 to 15, all different within a row; in each aligned block of 128 rows (0 to 127, 128 to 255, ...) at most 40 rows name the same one
- gates: float32 [32768, 4], P(('dp', 'expert')), may hold values from 0.05 to 1
- w_in: bfloat16 [16, 768, 2048], P('expert', 'tensor'), may hold values from -0.125 to 0.125
- w_out: bfloat16 [16, 768, 2048], P('expert', 'tensor'), may hold values from -0.21875 to 0.21875
- cotangent: bfloat16 [32768, 2048], P(('dp', 'expert'), 'tensor'), may hold values from -8 to 8
Outputs:
- mixed: bfloat16 [32768, 2048], P(('dp', 'expert'), 'tensor')
- grad_tokens: bfloat16 [32768, 2048], P(('dp', 'expert'), 'tensor')
- grad_gates: float32 [32768, 4], P(('dp', 'expert'))
- grad_in: float32 [16, 768, 2048], P('expert', 'tensor', 'dp')
- grad_out: float32 [16, 768, 2048], P('expert', 'tensor', 'dp')
Inputs may be any that keep to these rules, and one draw needn't show every extreme that they name: `routes`: each row names 4 different experts. The rows of one device (aligned blocks of 128 rows) name no expert more than 40 times, and in every draw some block names some expert exactly 40 times.
All inputs are finite; a program needn't handle non-finite values.
Results may differ from a plain program's by a relative error of at most 0.018.
Values may be sent and summed in bfloat16 or wider, within the bound.
A program may use at most 64 MiB of HBM per device.

v0:
```python
import jax
import jax.numpy as jnp
from jax import lax
from jax.sharding import PartitionSpec as P


def silu_slope(pre_value):
    logistic = jax.nn.sigmoid(pre_value)
    return logistic * (1.0 + pre_value * (1.0 - logistic))


def to_owner(slot_rows):
    return lax.all_to_all(slot_rows, "expert", split_axis=0, concat_axis=0, tiled=True)


def to_source(owner_rows):
    return lax.all_to_all(owner_rows, "expert", split_axis=0, concat_axis=0, tiled=True)


def core_halves(local_part):
    return lax.all_gather(local_part, "tensor", axis=3, tiled=True)


def per_device(tokens, routes, gates, w_in, w_out, cotangent):
    tok_count, top_count = routes.shape
    exp_local, hid_local, model_width = w_in.shape
    owners = lax.axis_size("expert")
    experts = exp_local * owners
    capacity = min(
        tok_count, ((tok_count * top_count * 5 + 4 * experts - 1) // (4 * experts) + 7) // 8 * 8
    )
    pair_count = tok_count * top_count
    half_width = tokens.shape[1]
    flat_routes = routes.reshape(pair_count)
    one_hot = (flat_routes[:, None] == jnp.arange(experts, dtype=jnp.int32)[None, :]).astype(
        jnp.int32
    )
    rank_before = jnp.cumsum(one_hot, axis=0) - one_hot
    slot_index = jnp.sum(rank_before * one_hot, axis=1)
    destination = flat_routes * capacity + slot_index
    source = (
        jnp.full((experts * capacity,), pair_count, jnp.int32)
        .at[destination]
        .set(jnp.arange(pair_count, dtype=jnp.int32))
    )
    source_row = source // top_count
    zero_row = jnp.zeros((1, half_width), tokens.dtype)
    tokens_pad = jnp.concatenate([tokens, zero_row], axis=0)
    cotangent_pad = jnp.concatenate([cotangent, zero_row], axis=0)
    gate_pad = jnp.concatenate([gates.reshape(pair_count), jnp.zeros((1,), jnp.float32)])
    w_in_cols, w_out_cols = (
        lax.all_to_all(w_in, "tensor", split_axis=2, concat_axis=1, tiled=True),
        lax.all_to_all(w_out, "tensor", split_axis=2, concat_axis=1, tiled=True),
    )
    rows_send = tokens_pad[source_row].reshape(experts, capacity, half_width)
    scaled = (gate_pad[source][:, None] * cotangent_pad[source_row].astype(jnp.float32)).astype(
        jnp.bfloat16
    )
    scaled_send = scaled.reshape(experts, capacity, half_width)
    received = to_owner(rows_send)
    grad_received = to_owner(scaled_send)
    received = received.reshape(owners, exp_local, capacity, half_width)
    grad_received = grad_received.reshape(owners, exp_local, capacity, half_width)
    rows_full = core_halves(received)
    pre_value = jnp.einsum("necd,efd->necf", rows_full, w_in, preferred_element_type=jnp.float32)
    hidden = jax.nn.silu(pre_value).astype(jnp.bfloat16)
    hidden_full = core_halves(hidden)
    expert_out = jnp.einsum(
        "necf,efd->necd", hidden_full, w_out_cols, preferred_element_type=jnp.float32
    ).astype(jnp.bfloat16)
    grad_full = core_halves(grad_received)
    grad_hidden = jnp.einsum("necd,efd->necf", grad_full, w_out, preferred_element_type=jnp.float32)
    grad_pre = (grad_hidden * silu_slope(pre_value)).astype(jnp.bfloat16)
    grad_pre_full = core_halves(grad_pre)
    grad_rows = jnp.einsum(
        "necf,efd->necd", grad_pre_full, w_in_cols, preferred_element_type=jnp.float32
    ).astype(jnp.bfloat16)
    out_send = expert_out.reshape(experts, capacity, half_width)
    back_send = grad_rows.reshape(experts, capacity, half_width)
    returned = to_source(out_send)
    grad_returned = to_source(back_send)
    returned = returned.reshape(experts * capacity, half_width)
    grad_returned = grad_returned.reshape(experts * capacity, half_width)
    picked = returned[destination].reshape(tok_count, top_count, half_width).astype(jnp.float32)
    mixed = jnp.sum(gates[:, :, None] * picked, axis=1).astype(jnp.bfloat16)
    cotangent_wide = cotangent.astype(jnp.float32)
    gate_part = jnp.sum(cotangent_wide[:, None, :] * picked, axis=2)
    grad_gates = lax.psum(gate_part, "tensor")
    gathered_back = (
        grad_returned[destination].reshape(tok_count, top_count, half_width).astype(jnp.float32)
    )
    grad_tokens = jnp.sum(gathered_back, axis=1).astype(jnp.bfloat16)
    block_part = rows_full
    grad_in_rows = lax.psum_scatter(
        jnp.einsum(
            "necd,necf->def", block_part, grad_pre, preferred_element_type=jnp.float32
        ).astype(jnp.bfloat16),
        "dp",
        scatter_dimension=0,
        tiled=True,
    ).astype(jnp.float32)
    block_part = grad_full
    grad_out_rows = lax.psum_scatter(
        jnp.einsum("necd,necf->def", block_part, hidden, preferred_element_type=jnp.float32).astype(
            jnp.bfloat16
        ),
        "dp",
        scatter_dimension=0,
        tiled=True,
    ).astype(jnp.float32)
    grad_in = jnp.transpose(grad_in_rows, (1, 2, 0))
    grad_out = jnp.transpose(grad_out_rows, (1, 2, 0))
    return (mixed, grad_tokens, grad_gates, grad_in, grad_out)


def solution(mesh):
    placed = (
        P(("dp", "expert"), "tensor"),
        P(("dp", "expert"), None),
        P(("dp", "expert"), None),
        P("expert", "tensor", None),
        P("expert", "tensor", None),
        P(("dp", "expert"), "tensor"),
    )
    return jax.shard_map(
        per_device,
        mesh=mesh,
        in_specs=placed,
        out_specs=(
            P(("dp", "expert"), "tensor"),
            P(("dp", "expert"), "tensor"),
            P(("dp", "expert"), None),
            P("expert", "tensor", "dp"),
            P("expert", "tensor", "dp"),
        ),
        check_vma=False,
    )
```

profile of v0, /device:TPU:160, one launch (start us, length us, event | category | flops | bytes accessed | tf_op | source)
XLA Modules:
  0.0 433.8 jit_solution(12156266584508027382)
XLA Ops:
  9.1 1.2 reduce-window.6
  10.6 2.4 scatter_custom_fusion
  14.1 3.5 gather_fusion
  17.6 14.0 %all-to-all-start = ((bf16[16,40,1024]{2,1,0:T(8,128)(2,1)}), bf16[16,40,1024]{2,1,0:T(8,128)(2,1)S(1)}, u32[]{:S(2)}, u32[]{:S(2)}) async-start(bf16[16,40,1024]{2,1,0:T(8,128)(2,1)} %bitcast.3), calls=%async_computation | async-start | bytes 2621440 | tf_op jit(solution)/shard_map/all_to_all | solution.py:13
  31.9 2.8 gather_fusion.2
  34.8 2.8 gather_fusion.3
  37.7 27.8 %all-to-all-done = bf16[16,40,1024]{2,1,0:T(8,128)(2,1)S(1)} async-done(((bf16[16,40,1024]{2,1,0:T(8,128)(2,1)}), bf16[16,40,1024]{2,1,0:T(8,128)(2,1)S(1)}, u32[]{:S(2)}, u32[]{:S(2)}) %all-to-all-start) | async-done | bytes 1310752 | tf_op jit(solution)/shard_map/all_to_all | solution.py:13
  65.5 1.1 copy-done
  66.9 40.7 %all_to_all.50 = bf16[16,40,1024]{2,1,0:T(8,128)(2,1)} all-to-all(bf16[16,40,1024]{2,1,0:T(8,128)(2,1)S(1)} %fusion), channel_id=1, replica_groups=mesh['dp'=16,'expert'=16,'tensor'=2] {'expert'}, dimensions={0} | all-to-all | bytes 2621440 | tf_op jit(solution)/shard_map/all_to_all | solution.py:13
  107.9 4.5 %multiply_convert_fusion = (bf16[16,1,40,384]{3,2,0,1:T(8,128)(2,1)}, f32[16,1,40,384]{3,2,0,1:T(8,128)}) fusion(bf16[16,40,2048]{2,1,0:T(8,128)(2,1)} %all-gather.5.cloned.1.call-done, bf16[1,384,2048]{2,1,0:T(8,128)(2,1)S(1)} %copy-done.6), kind=kOutput, calls=%fused_computation.26 | convolution fusion | flops 1007861760 | bytes 5668864 | tf_op jit(solution)/shard_map/necd,efd->necf/dot_general | solution.py:65
  112.5 32.0 %all-gather.7.cloned.1.call-done = bf16[16,40,2048]{2,1,0:T(8,128)(2,1)} async-done(((bf16[16,40,1024]{2,1,0:T(8,128)(2,1)}), bf16[16,40,2048]{2,1,0:T(8,128)(2,1)}) %all-gather.7.cloned.1.call-update) | async-done | bytes 2621456 | tf_op jit(solution)/shard_map/all_gather | solution.py:21
  144.4 3.8 fusion.16
  149.0 1.4 fusion.1
  150.4 1.6 copy.48
  152.1 7.9 %copy.41 = bf16[1,384,2048]{1,0,2:T(2,128)(2,1)S(1)} copy(bf16[1,384,2048]{2,1,0:T(8,128)(2,1)} %param.9) | data formatting | bytes 3145728 | tf_op args[3]
  160.5 34.4 %reduce.8 = bf16[2048,384]{1,0:T(8,128)(2,1)} reduce(bf16[2048,1,384]{2,1,0:T(2,128)(2,1)S(1)} %bitcast.127, bf16[]{:T(256)} %broadcast.98), dimensions={1}, to_apply=%bitcast.113.reduce_sub_computation | reduce | bytes 3145730
  195.0 2.6 reshape.238
  197.5 4.8 %all-to-all-start.4 = ((bf16[2,2,196608]{2,1,0:T(2,128)(2,1)}), bf16[2,2,196608]{2,1,0:T(2,128)(2,1)}, u32[]{:S(2)}, u32[]{:S(2)}) async-start(bf16[2,2,196608]{2,1,0:T(2,128)(2,1)} %reshape.238), calls=%async_computation.4 | async-start | bytes 3145728 | tf_op jit(solution)/shard_map/all_to_all | solution.py:52
  202.4 7.9 %copy.38 = bf16[1,384,2048]{1,0,2:T(2,128)(2,1)S(1)} copy(bf16[1,384,2048]{2,1,0:T(8,128)(2,1)} %param.10) | data formatting | bytes 3145728 | tf_op args[4]
  210.3 34.5 %reduce.7 = bf16[2048,384]{1,0:T(8,128)(2,1)} reduce(bf16[2048,1,384]{2,1,0:T(2,128)(2,1)S(1)} %bitcast.128, bf16[]{:T(256)} %broadcast.98), dimensions={1}, to_apply=%bitcast.111.reduce_sub_computation | reduce | bytes 3145730
  244.8 2.5 reshape.236
  247.3 4.6 %all-to-all-start.1 = ((bf16[2,2,196608]{2,1,0:T(2,128)(2,1)}), bf16[2,2,196608]{2,1,0:T(2,128)(2,1)}, u32[]{:S(2)}, u32[]{:S(2)}) async-start(bf16[2,2,196608]{2,1,0:T(2,128)(2,1)} %reshape.236), calls=%async_computation.1 | async-start | bytes 3145728 | tf_op jit(solution)/shard_map/all_to_all | solution.py:53
  251.9 2.5 reshape.239
  254.4 1.4 copy.53
  255.8 1.8 copy.42
  257.6 2.6 all_gather.15
  260.2 2.3 convolution_convert_fusion
  262.5 12.4 %all-to-all-start.5 = ((bf16[16,40,1024]{2,1,0:T(8,128)(2,1)}), bf16[16,40,1024]{2,1,0:T(8,128)(2,1)S(1)}, u32[]{:S(2)}, u32[]{:S(2)}) async-start(bf16[16,40,1024]{2,1,0:T(8,128)(2,1)} %convolution_convert_fusion), calls=%async_computation.5 | async-start | bytes 2621440 | tf_op jit(solution)/shard_map/all_to_all | solution.py:17
  275.0 3.6 reshape.237
  278.6 2.1 copy.52
  280.8 1.6 copy.39
  282.4 3.2 fusion.2
  285.6 1.6 copy.50
  287.2 2.9 all_gather.13
  290.1 2.3 convolution_convert_fusion.1
  292.4 18.1 %all-to-all-done.5 = bf16[16,40,1024]{2,1,0:T(8,128)(2,1)S(1)} async-done(((bf16[16,40,1024]{2,1,0:T(8,128)(2,1)}), bf16[16,40,1024]{2,1,0:T(8,128)(2,1)S(1)}, u32[]{:S(2)}, u32[]{:S(2)}) %all-to-all-start.5) | async-done | bytes 1310752 | tf_op jit(solution)/shard_map/all_to_all | solution.py:17
  310.5 12.5 %all-to-all-start.2 = ((bf16[16,40,1024]{2,1,0:T(8,128)(2,1)}), bf16[16,40,1024]{2,1,0:T(8,128)(2,1)S(1)}, u32[]{:S(2)}, u32[]{:S(2)}) async-start(bf16[16,40,1024]{2,1,0:T(8,128)(2,1)} %convolution_convert_fusion.1), calls=%async_computation.2 | async-start | bytes 2621440 | tf_op jit(solution)/shard_map/all_to_all | solution.py:17
  323.0 2.8 gather_fusion.4
  325.8 1.5 reshape.163
  327.2 2.1 reduce_sum.44
  329.3 23.0 %all-to-all-done.2 = bf16[16,40,1024]{2,1,0:T(8,128)(2,1)S(1)} async-done(((bf16[16,40,1024]{2,1,0:T(8,128)(2,1)}), bf16[16,40,1024]{2,1,0:T(8,128)(2,1)S(1)}, u32[]{:S(2)}, u32[]{:S(2)}) %all-to-all-start.2) | async-done | bytes 1310752 | tf_op jit(solution)/shard_map/all_to_all | solution.py:17
  352.3 2.8 gather_fusion.1
  355.1 1.7 reshape.166
  356.9 2.6 multiply_reduce_fusion
  359.4 3.6 psum.7
  363.7 1.0 copy.49
  365.4 60.2 %reduce-scatter.9.cloned.1.call-done = bf16[128,384]{1,0:T(8,128)(2,1)} async-done(((bf16[2048,384]{1,0:T(8,128)(2,1)}), bf16[128,384]{1,0:T(8,128)(2,1)}) %reduce-scatter.9.cloned.1.call-update) | async-done | bytes 98320
  425.6 1.0 copy.51
  (61 shorter events, 7.7 us)
Async XLA Ops:
  17.6 14.1 %copy-start.10 = (f32[128,4]{0,1:T(4,128)S(1)}, f32[128,4]{0,1:T(4,128)}, u32[]{:S(2)}) copy-start(f32[128,4]{0,1:T(4,128)} %param.8) | copy-start | bytes 6148
  17.6 47.9 %all-to-all-start = ((bf16[16,40,1024]{2,1,0:T(8,128)(2,1)}), bf16[16,40,1024]{2,1,0:T(8,128)(2,1)S(1)}, u32[]{:S(2)}, u32[]{:S(2)}) async-start(bf16[16,40,1024]{2,1,0:T(8,128)(2,1)} %bitcast.3), calls=%async_computation | async-start | bytes 2621440 | tf_op jit(solution)/shard_map/all_to_all | solution.py:13
  31.6 76.3 %all-gather.5.cloned.1.call-start = ((), (), s32[]{:S(2)}) async-start(), calls=%async_computation.8 | async-start | bytes 3932160 | tf_op jit(solution)/shard_map/all_gather | solution.py:21
  31.9 2.9 copy-start.8
  65.5 1.1 copy-start
  66.6 77.9 %all-gather.7.cloned.1.call-start = ((), (), s32[]{:S(2)}) async-start(), calls=%async_computation.9 | async-start | bytes 3932160 | tf_op jit(solution)/shard_map/all_gather | solution.py:21
  66.9 41.0 %copy-start.6 = (bf16[1,384,2048]{2,1,0:T(8,128)(2,1)S(1)}, bf16[1,384,2048]{2,1,0:T(8,128)(2,1)}, u32[]{:S(2)}) copy-start(bf16[1,384,2048]{2,1,0:T(8,128)(2,1)} %param.9) | copy-start | bytes 4718596
  107.7 36.8 %copy-start.7 = (bf16[1,384,2048]{2,1,0:T(8,128)(2,1)S(1)}, bf16[1,384,2048]{2,1,0:T(8,128)(2,1)}, u32[]{:S(2)}) copy-start(bf16[1,384,2048]{2,1,0:T(8,128)(2,1)} %param.10) | copy-start | bytes 4718596
  107.7 256.0 %reduce-scatter.7.cloned.1.call-start = ((), (), s32[]{:S(2)}) async-start(), calls=%async_computation.10 | async-start | bytes 1671168
  144.4 4.6 %copy-start.1 = (bf16[16,40,2048]{2,1,0:T(8,128)(2,1)S(1)}, bf16[16,40,2048]{2,1,0:T(8,128)(2,1)}, u32[]{:S(2)}) copy-start(bf16[16,40,2048]{2,1,0:T(8,128)(2,1)} %all-gather.5.cloned.1.call-done) | copy-start | bytes 7864324
  148.2 0.8 copy-start.3
  197.5 49.8 %all-to-all-start.4 = ((bf16[2,2,196608]{2,1,0:T(2,128)(2,1)}), bf16[2,2,196608]{2,1,0:T(2,128)(2,1)}, u32[]{:S(2)}, u32[]{:S(2)}) async-start(bf16[2,2,196608]{2,1,0:T(2,128)(2,1)} %reshape.238), calls=%async_computation.4 | async-start | bytes 3145728 | tf_op jit(solution)/shard_map/all_to_all | solution.py:52
  247.3 15.2 %all-to-all-start.1 = ((bf16[2,2,196608]{2,1,0:T(2,128)(2,1)}), bf16[2,2,196608]{2,1,0:T(2,128)(2,1)}, u32[]{:S(2)}, u32[]{:S(2)}) async-start(bf16[2,2,196608]{2,1,0:T(2,128)(2,1)} %reshape.236), calls=%async_computation.1 | async-start | bytes 3145728 | tf_op jit(solution)/shard_map/all_to_all | solution.py:53
  255.8 1.8 copy-start.4
  262.5 47.9 %all-to-all-start.5 = ((bf16[16,40,1024]{2,1,0:T(8,128)(2,1)}), bf16[16,40,1024]{2,1,0:T(8,128)(2,1)S(1)}, u32[]{:S(2)}, u32[]{:S(2)}) async-start(bf16[16,40,1024]{2,1,0:T(8,128)(2,1)} %convolution_convert_fusion), calls=%async_computation.5 | async-start | bytes 2621440 | tf_op jit(solution)/shard_map/all_to_all | solution.py:17
  274.9 150.6 %reduce-scatter.9.cloned.1.call-start = ((), (), s32[]{:S(2)}) async-start(), calls=%async_computation.11 | async-start | bytes 1671168
  280.7 1.7 copy-start.2
  287.2 2.9 copy-start.5
  292.4 30.5 %copy-start.9 = (bf16[128,1024]{1,0:T(8,128)(2,1)S(1)}, bf16[128,1024]{1,0:T(8,128)(2,1)}, u32[]{:S(2)}) copy-start(bf16[128,1024]{1,0:T(8,128)(2,1)} %param.11) | copy-start | bytes 786436
  310.5 41.9 %all-to-all-start.2 = ((bf16[16,40,1024]{2,1,0:T(8,128)(2,1)}), bf16[16,40,1024]{2,1,0:T(8,128)(2,1)S(1)}, u32[]{:S(2)}, u32[]{:S(2)}) async-start(bf16[16,40,1024]{2,1,0:T(8,128)(2,1)} %convolution_convert_fusion.1), calls=%async_computation.2 | async-start | bytes 2621440 | tf_op jit(solution)/shard_map/all_to_all | solution.py:17
Sparse Core Ops, SparseCore 0:
  66.7 36.6 all-gather.4
  107.8 36.6 all-gather.6
  152.2 90.8 reduce-scatter.6
  287.3 138.2 reduce-scatter.8
where the time goes:
time: 435 us; the launch traced here: 434 us
  waiting for transfers between devices  161 us (37%)
  other arithmetic  77.3 us (18%)
  local copies, waits for them, and re-layouts  65.3 us (15%)
  blocking collectives  49.8 us (11%)
  starting transfers between devices  48.6 us (11%)
  matrix products  17.5 us (4%)
  between operations  14.1 us (3%)
    unnamed x2, other arithmetic  68.9 us
    unnamed x6, waiting for transfers between devices  60.3 us
    all_to_all x2, waiting for transfers between devices, to_source(): lax.all_to_all(owner_rows, 'expert', split_axis=0, concat_axis=0, tiled=T...  41.1 us
    all_to_all x1, blocking collectives, to_owner(): lax.all_to_all(slot_rows, 'expert', split_axis=0, concat_axis=0, tiled=True)  40.7 us
    unnamed x38, local copies, waits for them, and re-layouts  39.8 us
    all_gather x2, waiting for transfers between devices, core_halves(): return lax.all_gather(local_part, 'tensor', axis=3, tiled=True)  32 us
    all_to_all x1, waiting for transfers between devices, to_owner(): lax.all_to_all(slot_rows, 'expert', split_axis=0, concat_axis=0, tiled=True)  27.8 us
    all_to_all x2, starting transfers between devices, to_source(): lax.all_to_all(owner_rows, 'expert', split_axis=0, concat_axis=0, tiled=T...  24.9 us
  transfers between devices with their start and end apart: 9, of which 5 were waited for; matrix products, arithmetic and copies ran while one was open for 32% of the time, Pallas kernels for 0%

commit v1 on v0

v1 whole, which is shorter than its diff:
```python
import functools

import jax
import jax.numpy as jnp
from jax import lax
from jax.experimental import pallas as pl
from jax.experimental.pallas import tpu as pltpu
from jax.sharding import PartitionSpec as P

MESH = pl.DeviceIdType.MESH
F32, BF16 = jnp.float32, jnp.bfloat16

NX, NYL = 4, 4
NZ, NYH = 8, 2
TOK = 128
CAP = 40
HEAD = 32
SLOTS = 2 * CAP
ROWS = NZ * SLOTS
HALF = 1024
HID = 384
CHUNKS = 4

PH_TOK_HEAD, PH_TOK_REST, PH_SCALED, PH_OUT, PH_BACK = 0, 1, 2, 3, 4
PHASES = PH_BACK + CHUNKS
SB_WIN, SB_WOUT, SB_ROWS, SB_HID, SB_SCALED, SB_PRE, SB_GATE = range(7)
YP_ROUTES, YP_GATES, YP_TOK, YP_COT, YP_MIX, YP_GG, YP_BACK = range(7)


def dot(a, b, dims):
    return lax.dot_general(a, b, (dims, ((), ())), preferred_element_type=F32)


NN = ((1,), (0,))
NT = ((1,), (1,))


def kernel(
    tok_ref, cot_ref, rt_ref, gt_ref, win_ref, wout_ref,
    mix_ref, gtok_ref, gg_ref, gin_ref, gout_ref,
    tok2, cot2, rt2, gt2, sel, rankm, gatem,
    send_tok, send_sc, rows, scal, hid, pre, slope, wi, wo,
    out, back, rout, rback, g_hi, g_lo, sel_t, hid_t, pre_t,
    mixo, mixs, mixr, bko, bks, bkr, ggp, ggs, ggr, ggm, ggx,
    part, xa, xb, xs, x1, x2, xd1, xd2, xq, xqb, yr,
    zs, zr, ss, sr, ps, pr, xsm, xrm, ys, yrm,
):
    dp = lax.axis_index("dp")
    ex = lax.axis_index("expert")
    c = lax.axis_index("tensor")
    x, yl = dp // NYL, dp % NYL
    z, yh = ex // NYH, ex % NYH
    sib = {"tensor": 1 - c}
    mirror = {"dp": x * NYL + (NYL - 1 - yl), "expert": z * NYH + (1 - yh)}
    x_up = {"dp": ((x + 1) % NX) * NYL + yl}
    x_dn = {"dp": ((x + NX - 1) % NX) * NYL + yl}

    def z_dev(other):
        return {"expert": other * NYH + yh}

    def y_dev(other):
        return {"dp": x * NYL + other}

    def rcopy(src, dst, send, recv, dev):
        return pltpu.make_async_remote_copy(
            src_ref=src, dst_ref=dst, send_sem=send, recv_sem=recv,
            device_id=dev, device_id_type=MESH,
        )

    barrier = pltpu.get_barrier_semaphore()

    def greet(dev):
        pl.semaphore_signal(barrier, inc=1, device_id=dev, device_id_type=MESH)

    for step in range(1, NZ):
        greet(z_dev((z + step) % NZ))
    for step in range(1, NYL):
        greet(y_dev((yl + step) % NYL))
    greet(sib)
    greet(mirror)
    greet(x_up)
    greet(x_dn)

    tok2[0:TOK, :] = tok_ref[...]
    cot2[0:TOK, :] = cot_ref[...]
    rt2[:, 0:TOK] = rt_ref[...]
    gt2[:, 0:TOK] = gt_ref[...]
    before = (
        lax.broadcasted_iota(jnp.int32, (TOK, TOK), 0)
        < lax.broadcasted_iota(jnp.int32, (TOK, TOK), 1)
    ).astype(F32).astype(BF16)
    names = 2 * lax.broadcasted_iota(jnp.int32, (16, TOK), 0) + yh

    def place(block):
        cols = slice(block * TOK, (block + 1) * TOK)
        hits = jnp.zeros((16, TOK), F32)
        gate = jnp.zeros((16, TOK), F32)
        for k in range(4):
            hit = rt2[k : k + 1, cols] == names
            hits = hits + jnp.where(hit, 1.0, 0.0)
            gate = gate + jnp.where(hit, gt2[k : k + 1, cols], 0.0)
        rank = dot(hits.astype(BF16), before, NN)
        rank = jnp.where(hits > 0.0, rank, -5.0)
        for e in range(NZ):
            rankm[e, :, cols] = rank[e : e + 1]
            gatem[e, :, cols] = gate[e : e + 1]

    place(0)
    head_slot = lax.broadcasted_iota(jnp.int32, (HEAD, TOK), 0).astype(F32)

    def own_head(e, carry):
        choose = jnp.where(rankm[e, :, 0:TOK] == head_slot, 1.0, 0.0).astype(BF16)
        at = pl.multiple_of(e * SLOTS, 16)
        send_tok[pl.ds(at, HEAD), :] = dot(choose, tok2[0:TOK, :], NN).astype(BF16)
        return carry

    lax.fori_loop(0, NZ, own_head, 0)

    pl.semaphore_wait(barrier, (NZ - 1) + (NYL - 1) + 4)

    y_in = [
        rcopy(rt_ref, rt2.at[:, pl.ds(TOK, TOK)], ps.at[YP_ROUTES], pr.at[YP_ROUTES], mirror),
        rcopy(gt_ref, gt2.at[:, pl.ds(TOK, TOK)], ps.at[YP_GATES], pr.at[YP_GATES], mirror),
        rcopy(tok_ref, tok2.at[pl.ds(TOK, TOK), :], ps.at[YP_TOK], pr.at[YP_TOK], mirror),
        rcopy(cot_ref, cot2.at[pl.ds(TOK, TOK), :], ps.at[YP_COT], pr.at[YP_COT], mirror),
    ]
    for cp in y_in:
        cp.start()

    def z_copy(src, dst, lo, size, cols, phase, other, sender):
        s_at = pl.multiple_of(other * SLOTS + lo, 16)
        d_at = pl.multiple_of(sender * SLOTS + lo, 16)
        return rcopy(
            src.at[pl.ds(s_at, size), cols], dst.at[pl.ds(d_at, size), cols],
            zs.at[phase, other], zr.at[phase, sender], z_dev(other),
        )

    full = pl.ds(0, HALF)

    def z_send(src, dst, lo, size, cols, phase):
        def one(step, carry):
            z_copy(src, dst, lo, size, cols, phase, (z + step) % NZ, z).start()
            return carry

        lax.fori_loop(1, NZ, one, 0)

    def z_recv(src, dst, lo, size, cols, phase):
        def one(step, carry):
            other = (z + step) % NZ
            z_copy(src, dst, lo, size, cols, phase, other, other).wait_recv()
            return carry

        lax.fori_loop(1, NZ, one, 0)

    def z_sent(src, dst, lo, size, cols, phase):
        def one(step, carry):
            z_copy(src, dst, lo, size, cols, phase, (z + step) % NZ, z).wait_send()
            return carry

        lax.fori_loop(1, NZ, one, 0)

    here = pl.ds(pl.multiple_of(z * SLOTS, 16), SLOTS)
    rows_own, scal_own = rows.at[c], scal.at[c]
    z_send(send_tok, rows_own, 0, HEAD, full, PH_TOK_HEAD)

    w_other = pl.ds(pl.multiple_of((1 - c) * HALF, 128), HALF)
    w_mine = pl.ds(pl.multiple_of(c * HALF, 128), HALF)
    w_cp = [
        rcopy(win_ref.at[:, w_other], wi.at[c], ss.at[SB_WIN], sr.at[SB_WIN], sib),
        rcopy(wout_ref.at[:, w_other], wo.at[c], ss.at[SB_WOUT], sr.at[SB_WOUT], sib),
    ]
    for cp in w_cp:
        cp.start()
    wi[c] = win_ref[:, w_mine]
    wo[c] = wout_ref[:, w_mine]

    r_id = lax.broadcasted_iota(jnp.int32, (SLOTS, 2 * TOK), 0)
    t_id = lax.broadcasted_iota(jnp.int32, (SLOTS, 2 * TOK), 1)
    late = jnp.where(t_id >= TOK, 1, 0)
    second = jnp.where(
        r_id < 2 * HEAD,
        jnp.where(r_id >= HEAD, 1, 0),
        jnp.where(r_id >= HEAD + CAP, 1, 0),
    )
    slot = jnp.where(
        r_id < HEAD, r_id, jnp.where(r_id < HEAD + CAP, r_id - HEAD, r_id - CAP)
    )
    slot_map = jnp.where(second == late, slot, -1).astype(F32)

    y_in[0].wait_recv()
    y_in[1].wait_recv()
    place(1)
    y_in[2].wait_recv()

    def gather_tok(e, carry):
        choose = jnp.where(rankm[e] == slot_map, 1.0, 0.0)
        at = pl.multiple_of(e * SLOTS, 16)
        sel[pl.ds(at, SLOTS), :] = choose
        send_tok[pl.ds(at + HEAD, SLOTS - HEAD), :] = dot(
            choose[HEAD:].astype(BF16), tok2[...], NN
        ).astype(BF16)
        return carry

    lax.fori_loop(0, NZ, gather_tok, 0)
    z_send(send_tok, rows_own, HEAD, SLOTS - HEAD, full, PH_TOK_REST)
    rows[c, here, :] = send_tok[here, :]

    y_in[3].wait_recv()

    def gather_cot(e, carry):
        at = pl.ds(pl.multiple_of(e * SLOTS, 16), SLOTS)
        choose = sel[at, :]
        gate = jnp.sum(choose * gatem[e], axis=1, keepdims=True)
        send_sc[at, :] = (gate * dot(choose.astype(BF16), cot2[...], NN)).astype(BF16)
        return carry

    lax.fori_loop(0, NZ, gather_cot, 0)
    z_send(send_sc, scal_own, 0, SLOTS, full, PH_SCALED)
    scal[c, here, :] = send_sc[here, :]

    def gates_of(e, carry):
        at = pl.ds(pl.multiple_of(e * SLOTS, 16), SLOTS)
        out_gate = sel[at, :] * gatem[e]
        slope[at, 0 : 2 * TOK] = out_gate
        return carry

    lax.fori_loop(0, NZ, gates_of, 0)

    def turn(i, carry):
        at = pl.ds(pl.multiple_of(i * 128, 128), 128)
        g_t = slope[at, 0 : 2 * TOK].T
        hi = g_t.astype(BF16)
        g_hi[:, at] = hi
        g_lo[:, at] = (g_t - hi.astype(F32)).astype(BF16)
        sel_t[:, at] = sel[at, :].T.astype(BF16)
        return carry

    lax.fori_loop(0, ROWS // 128, turn, 0)

    z_recv(send_tok, rows_own, 0, HEAD, full, PH_TOK_HEAD)
    z_recv(send_tok, rows_own, HEAD, SLOTS - HEAD, full, PH_TOK_REST)
    cp_rows = rcopy(rows.at[c], rows.at[c], ss.at[SB_ROWS], sr.at[SB_ROWS], sib)
    cp_rows.start()
    cp_rows.wait_recv()

    TILE = 320

    def tile(i):
        return pl.ds(pl.multiple_of(i * TILE, 64), TILE)

    def forward(i, carry):
        at = tile(i)
        v = dot(rows[0, at, :], win_ref[:, 0:HALF], NT) + dot(
            rows[1, at, :], win_ref[:, HALF:], NT
        )
        s = 1.0 / (1.0 + jnp.exp(-v))
        hid[c, at, :] = (v * s).astype(BF16)
        slope[at, :] = s * (1.0 + v * (1.0 - s))
        return carry

    lax.fori_loop(0, ROWS // TILE, forward, 0)
    cp_hid = rcopy(hid.at[c], hid.at[c], ss.at[SB_HID], sr.at[SB_HID], sib)
    cp_hid.start()
    w_cp[0].wait_recv()
    w_cp[1].wait_recv()
    cp_hid.wait_recv()

    def project(i, carry):
        at = tile(i)
        out[at, :] = (dot(hid[0, at, :], wo[0], NN) + dot(hid[1, at, :], wo[1], NN)).astype(BF16)
        return carry

    lax.fori_loop(0, ROWS // TILE, project, 0)
    z_send(out, rout, 0, SLOTS, full, PH_OUT)
    rout[here, :] = out[here, :]

    z_recv(send_sc, scal_own, 0, SLOTS, full, PH_SCALED)
    cp_sc = rcopy(scal.at[c], scal.at[c], ss.at[SB_SCALED], sr.at[SB_SCALED], sib)
    cp_sc.start()
    cp_sc.wait_recv()

    def backward(i, carry):
        at = tile(i)
        v = dot(scal[0, at, :], wout_ref[:, 0:HALF], NT) + dot(
            scal[1, at, :], wout_ref[:, HALF:], NT
        )
        pre[c, at, :] = (v * slope[at, :]).astype(BF16)
        return carry

    lax.fori_loop(0, ROWS // TILE, backward, 0)
    cp_pre = rcopy(pre.at[c], pre.at[c], ss.at[SB_PRE], sr.at[SB_PRE], sib)
    cp_pre.start()
    cp_pre.wait_recv()

    def project_back(i, carry):
        at = tile(i)
        back[at, :] = (dot(pre[0, at, :], wi[0], NN) + dot(pre[1, at, :], wi[1], NN)).astype(BF16)
        return carry

    lax.fori_loop(0, ROWS // TILE, project_back, 0)
    WIDE = HALF // CHUNKS

    def piece(q):
        return pl.ds(q * WIDE, WIDE)

    for q in range(CHUNKS):
        z_send(back, rback, 0, SLOTS, piece(q), PH_BACK + q)
    rback[here, :] = back[here, :]

    def flip(i, carry):
        at = pl.ds(pl.multiple_of(i * 128, 128), 128)
        hid_t[:, at] = hid[c, at, :].astype(F32).T.astype(BF16)
        pre_t[:, at] = pre[c, at, :].astype(F32).T.astype(BF16)
        return carry

    lax.fori_loop(0, ROWS // 128, flip, 0)
    for h in range(2):
        def weigh(n, carry, h=h):
            src = pl.ds(pl.multiple_of(n * 256, 256), 256)
            dst = pl.ds(pl.multiple_of(h * HALF + n * 256, 256), 256)
            part[0:HID, dst] = dot(pre_t[...], rows[h, :, src], NN).astype(BF16)
            part[HID:, dst] = dot(hid_t[...], scal[h, :, src], NN).astype(BF16)
            return carry

        lax.fori_loop(0, HALF // 256, weigh, 0)

    XW = 512
    XH = XW // 2

    def x_cols(other, half):
        return pl.ds(pl.multiple_of(other * XW + half * XH, 256), XH)

    up, dn, far = (x + 1) % NX, (x + NX - 1) % NX, (x + 2) % NX
    x_first = [
        rcopy(part.at[:, x_cols(far, 0)], xa, xsm.at[0], xrm.at[0], x_up),
        rcopy(part.at[:, x_cols(far, 1)], xb, xsm.at[1], xrm.at[1], x_dn),
        rcopy(part.at[:, x_cols(up, 1)], xd1, xsm.at[2], xrm.at[2], x_up),
        rcopy(part.at[:, x_cols(dn, 0)], xd2, xsm.at[3], xrm.at[3], x_dn),
    ]
    for cp in x_first:
        cp.start()
    x_first[0].wait_recv()
    xs[0] = (part[:, x_cols(up, 0)].astype(F32) + xa[...].astype(F32)).astype(BF16)
    x_first[1].wait_recv()
    xs[1] = (part[:, x_cols(dn, 1)].astype(F32) + xb[...].astype(F32)).astype(BF16)
    x_second = [
        rcopy(xs.at[0], x1, xsm.at[4], xrm.at[4], x_up),
        rcopy(xs.at[1], x2, xsm.at[5], xrm.at[5], x_dn),
    ]
    for cp in x_second:
        cp.start()

    z_recv(out, rout, 0, SLOTS, full, PH_OUT)

    def mix(n, carry):
        at = pl.ds(pl.multiple_of(n * 256, 256), 256)
        m = dot(g_hi[...], rout[:, at], NN) + dot(g_lo[...], rout[:, at], NN)
        mixo[:, at] = m[0:TOK]
        mixs[:, at] = m[TOK:].astype(BF16)
        return carry

    lax.fori_loop(0, HALF // 256, mix, 0)
    cp_mix = rcopy(mixs, mixr, ps.at[YP_MIX], pr.at[YP_MIX], mirror)
    cp_mix.start()

    def inner(e, acc):
        at = pl.ds(pl.multiple_of(e * SLOTS, 16), SLOTS)
        dots = dot(rout[at, :], cot2[...], NT) * sel[at, :]
        per_token = jnp.sum(dots, axis=0, keepdims=True)
        hit = rt2[...] == 2 * e + yh
        return acc + jnp.where(hit, per_token, 0.0)

    gate_part = lax.fori_loop(0, NZ, inner, jnp.zeros((4, 2 * TOK), F32))
    ggp[...] = gate_part[:, 0:TOK]
    ggs[...] = gate_part[:, TOK:]
    cp_gg = rcopy(ggs, ggr, ps.at[YP_GG], pr.at[YP_GG], mirror)
    cp_gg.start()

    x_first[2].wait_recv()
    x_first[3].wait_recv()
    x_second[0].wait_recv()
    x_second[1].wait_recv()
    xq[:, 0:XH] = (
        part[:, x_cols(x, 0)].astype(F32) + x1[...].astype(F32) + xd2[...].astype(F32)
    )
    xq[:, XH:] = (
        part[:, x_cols(x, 1)].astype(F32) + x2[...].astype(F32) + xd1[...].astype(F32)
    )
    xqb[...] = xq[...].astype(BF16)

    def y_cols(other):
        return pl.ds(pl.multiple_of(other * 128, 128), 128)

    def y_copy(other, sender):
        return rcopy(xqb.at[:, y_cols(other)], yr.at[sender], ys.at[other], yrm.at[sender], y_dev(other))

    for step in range(1, NYL):
        y_copy((yl + step) % NYL, yl).start()

    cp_gg.wait_recv()
    ggm[...] = ggp[...] + ggr[...]
    cp_gs = rcopy(ggm, ggx, ss.at[SB_GATE], sr.at[SB_GATE], sib)
    cp_gs.start()
    cp_mix.wait_recv()
    mix_ref[...] = (mixo[...] + mixr[...].astype(F32)).astype(BF16)
    cp_gs.wait_recv()
    gg_ref[...] = ggm[...] + ggx[...]

    total = xq[:, y_cols(yl)]
    for step in range(1, NYL):
        other = (yl + step) % NYL
        y_copy(other, other).wait_recv()
        total = total + yr[other].astype(F32)
    gin_ref[...] = total[0:HID]
    gout_ref[...] = total[HID:]

    cp_back = []
    for q in range(CHUNKS):
        z_recv(back, rback, 0, SLOTS, piece(q), PH_BACK + q)
        b = dot(sel_t[...], rback[:, piece(q)], NN)
        bko[:, piece(q)] = b[0:TOK]
        bks[:, piece(q)] = b[TOK:].astype(BF16)
        cp = rcopy(
            bks.at[:, piece(q)], bkr.at[:, piece(q)],
            ps.at[YP_BACK + q], pr.at[YP_BACK + q], mirror,
        )
        cp.start()
        cp_back.append(cp)
    for q in range(CHUNKS):
        cp_back[q].wait_recv()
        gtok_ref[:, piece(q)] = (bko[:, piece(q)] + bkr[:, piece(q)].astype(F32)).astype(BF16)

    z_sent(send_tok, rows_own, 0, HEAD, full, PH_TOK_HEAD)
    z_sent(send_tok, rows_own, HEAD, SLOTS - HEAD, full, PH_TOK_REST)
    z_sent(send_sc, scal_own, 0, SLOTS, full, PH_SCALED)
    z_sent(out, rout, 0, SLOTS, full, PH_OUT)
    for q in range(CHUNKS):
        z_sent(back, rback, 0, SLOTS, piece(q), PH_BACK + q)
    for step in range(1, NYL):
        y_copy((yl + step) % NYL, yl).wait_send()
    for cp in y_in + w_cp + x_first + x_second + cp_back:
        cp.wait_send()
    for cp in (cp_rows, cp_hid, cp_sc, cp_pre, cp_mix, cp_gg, cp_gs):
        cp.wait_send()


def per_device(tokens, routes, gates, w_in, w_out, cotangent):
    vmem = pl.BlockSpec(memory_space=pltpu.VMEM)
    V = pltpu.VMEM
    dma = pltpu.SemaphoreType.DMA
    outs = pl.pallas_call(
        kernel,
        out_shape=(
            jax.ShapeDtypeStruct((TOK, HALF), BF16),
            jax.ShapeDtypeStruct((TOK, HALF), BF16),
            jax.ShapeDtypeStruct((4, TOK), F32),
            jax.ShapeDtypeStruct((HID, 128), F32),
            jax.ShapeDtypeStruct((HID, 128), F32),
        ),
        in_specs=[vmem] * 6,
        out_specs=(vmem,) * 5,
        scratch_shapes=[
            V((2 * TOK, HALF), BF16), V((2 * TOK, HALF), BF16),
            V((4, 2 * TOK), jnp.int32), V((4, 2 * TOK), F32),
            V((ROWS, 2 * TOK), F32), V((NZ, 1, 2 * TOK), F32), V((NZ, 1, 2 * TOK), F32),
            V((ROWS, HALF), BF16), V((ROWS, HALF), BF16),
            V((2, ROWS, HALF), BF16), V((2, ROWS, HALF), BF16),
            V((2, ROWS, HID), BF16), V((2, ROWS, HID), BF16), V((ROWS, HID), F32),
            V((2, HID, HALF), BF16), V((2, HID, HALF), BF16),
            V((ROWS, HALF), BF16), V((ROWS, HALF), BF16),
            V((ROWS, HALF), BF16), V((ROWS, HALF), BF16),
            V((2 * TOK, ROWS), BF16), V((2 * TOK, ROWS), BF16), V((2 * TOK, ROWS), BF16),
            V((HID, ROWS), BF16), V((HID, ROWS), BF16),
            V((TOK, HALF), F32), V((TOK, HALF), BF16), V((TOK, HALF), BF16),
            V((TOK, HALF), F32), V((TOK, HALF), BF16), V((TOK, HALF), BF16),
            V((4, TOK), F32), V((4, TOK), F32), V((4, TOK), F32),
            V((4, TOK), F32), V((4, TOK), F32),
            V((2 * HID, 2 * HALF), BF16),
            V((2 * HID, 256), BF16), V((2 * HID, 256), BF16), V((2, 2 * HID, 256), BF16),
            V((2 * HID, 256), BF16), V((2 * HID, 256), BF16),
            V((2 * HID, 256), BF16), V((2 * HID, 256), BF16),
            V((2 * HID, 512), F32), V((2 * HID, 512), BF16),
            V((NYL, 2 * HID, 128), BF16),
            dma((PHASES, NZ)), dma((PHASES, NZ)), dma((7,)), dma((7,)),
            dma((YP_BACK + CHUNKS,)), dma((YP_BACK + CHUNKS,)),
            dma((6,)), dma((6,)), dma((NYL,)), dma((NYL,)),
        ],
        compiler_params=pltpu.CompilerParams(
            collective_id=0, has_side_effects=True, vmem_limit_bytes=60 * 1024 * 1024
        ),
    )(tokens, cotangent, routes.T, gates.T, w_in[0], w_out[0])
    mixed, grad_tokens, grad_gates, grad_in, grad_out = outs
    return mixed, grad_tokens, grad_gates.T, grad_in[None], grad_out[None]


def solution(mesh):
    placed = (
        P(("dp", "expert"), "tensor"),
        P(("dp", "expert"), None),
        P(("dp", "expert"), None),
        P("expert", "tensor", None),
        P("expert", "tensor", None),
        P(("dp", "expert"), "tensor"),
    )
    return jax.shard_map(
        per_device,
        mesh=mesh,
        in_specs=placed,
        out_specs=(
            P(("dp", "expert"), "tensor"),
            P(("dp", "expert"), "tensor"),
            P(("dp", "expert"), None),
            P("expert", "tensor", "dp"),
            P("expert", "tensor", "dp"),
        ),
        check_vma=False,
    )
```

time: 435 us -> 165 us (0.38)
  the two profiles are of different devices: /device:TPU:160 before, /device:TPU:104 now
where the time goes in v1:
time: 165 us
  Pallas kernels  157 us (95%)
  local copies, waits for them, and re-layouts  6.92 us (4%)
    pallas_call x1, Pallas kernels, per_device(): pl.pallas_call(kernel, out_shape=(jax.ShapeDtypeStruct((TOK, HALF), BF16)...  157 us
    unnamed x7, local copies, waits for them, and re-layouts  6.92 us

profile of v1, /device:TPU:104, one launch (start us, length us, event | category | flops | bytes accessed | tf_op | source)
XLA Modules:
  0.0 164.8 jit_solution(2654695112606506821)
XLA Ops:
  0.6 157.3 %shard_map.101 = (bf16[128,1024]{1,0:T(8,128)(2,1)}, bf16[128,1024]{1,0:T(8,128)(2,1)}, f32[4,128]{1,0:T(4,128)}, f32[384,128]{1,0:T(8,128)}, f32[384,128]{1,0:T(8,128)}) custom-call(bf16[128,1024]{1,0:T(8,128)(2,1)} %tok_ref.1, bf16[128,1024]{1,0:T(8,128)(2,1)} %cot_ref.1, s32[4,128]{1,0:T(4,128)} %bitcast.11, f32[4,128]{1,0:T(4,128)} %bitcast.12, ...), custom_call_target="tpu_custom_call" | custom-call | tf_op jit(solution)/shard_map/pallas_call | solution.py:451
  157.9 0.0 copy-start
  157.9 1.7 %copy.16 = bf16[128,1024]{1,0:T(8,128)(2,1)} copy(bf16[128,1024]{1,0:T(8,128)(2,1)} %get-tuple-element.20) | data formatting | bytes 524288
  159.6 1.7 %copy.17 = bf16[128,1024]{1,0:T(8,128)(2,1)} copy(bf16[128,1024]{1,0:T(8,128)(2,1)} %get-tuple-element.21) | data formatting | bytes 524288
  161.3 1.2 copy.18
  162.5 1.6 copy.19
  164.1 0.0 copy-done
  164.1 0.7 copy.20
Async XLA Ops:
  157.9 6.2 %copy-start = (f32[384,128]{1,0:T(8,128)S(1)}, f32[384,128]{1,0:T(8,128)}, u32[]{:S(2)}) copy-start(f32[384,128]{1,0:T(8,128)} %get-tuple-element.14) | copy-start | bytes 589828

commit v2 on v1

--- a/solution.py
+++ b/solution.py
@@ -19,11 +19,12 @@
 ROWS = NZ * SLOTS
 HALF = 1024
 HID = 384
-CHUNKS = 4
-
-PH_TOK_HEAD, PH_TOK_REST, PH_SCALED, PH_OUT, PH_BACK = 0, 1, 2, 3, 4
+PIECES = ((0, 512), (512, 256), (768, 128), (896, 128))
+CHUNKS = len(PIECES)
+
+PH_TOK_HEAD, PH_TOK_REST, PH_SC_HEAD, PH_SC_REST, PH_OUT, PH_BACK = range(6)
 PHASES = PH_BACK + CHUNKS
-SB_WIN, SB_WOUT, SB_ROWS, SB_HID, SB_SCALED, SB_PRE, SB_GATE = range(7)
+SB_WIN, SB_WOUT, SB_HID, SB_PRE, SB_GATE = range(5)
 YP_ROUTES, YP_GATES, YP_TOK, YP_COT, YP_MIX, YP_GG, YP_BACK = range(7)
 
 
@@ -36,14 +37,14 @@
 
 
 def kernel(
-    tok_ref, cot_ref, rt_ref, gt_ref, win_ref, wout_ref,
+    tok_in, cot_in, rt_in, gt_in, win_in, wout_in,
     mix_ref, gtok_ref, gg_ref, gin_ref, gout_ref,
-    tok2, cot2, rt2, gt2, sel, rankm, gatem,
+    tok2, cot2, rt2, gt2, win_ref, wout_ref, sel, rankm, gatem,
     send_tok, send_sc, rows, scal, hid, pre, slope, wi, wo,
     out, back, rout, rback, g_hi, g_lo, sel_t, hid_t, pre_t,
     mixo, mixs, mixr, bko, bks, bkr, ggp, ggs, ggr, ggm, ggx,
     part, xa, xb, xs, x1, x2, xd1, xd2, xq, xqb, yr,
-    zs, zr, ss, sr, ps, pr, xsm, xrm, ys, yrm,
+    zs, zr, ss, sr, hs, hr, ps, pr, xsm, xrm, ys, yrm, ls,
 ):
     dp = lax.axis_index("dp")
     ex = lax.axis_index("expert")
@@ -81,10 +82,26 @@
     greet(x_up)
     greet(x_dn)
 
-    tok2[0:TOK, :] = tok_ref[...]
-    cot2[0:TOK, :] = cot_ref[...]
-    rt2[:, 0:TOK] = rt_ref[...]
-    gt2[:, 0:TOK] = gt_ref[...]
+    w_other = pl.ds(pl.multiple_of((1 - c) * HALF, 128), HALF)
+    w_mine = pl.ds(pl.multiple_of(c * HALF, 128), HALF)
+    own = pl.ds(0, TOK)
+    local = [
+        pltpu.make_async_copy(src, dst, ls.at[i])
+        for i, (src, dst) in enumerate((
+            (rt_in, rt2.at[:, own]),
+            (gt_in, gt2.at[:, own]),
+            (tok_in, tok2.at[own, :]),
+            (cot_in, cot2.at[own, :]),
+            (win_in, win_ref),
+            (wout_in, wout_ref),
+            (win_in.at[:, w_mine], wi.at[c]),
+            (wout_in.at[:, w_mine], wo.at[c]),
+        ))
+    ]
+    for cp in local:
+        cp.start()
+    local[0].wait()
+    local[1].wait()
     before = (
         lax.broadcasted_iota(jnp.int32, (TOK, TOK), 0)
         < lax.broadcasted_iota(jnp.int32, (TOK, TOK), 1)
@@ -106,6 +123,7 @@
             gatem[e, :, cols] = gate[e : e + 1]
 
     place(0)
+    local[2].wait()
     head_slot = lax.broadcasted_iota(jnp.int32, (HEAD, TOK), 0).astype(F32)
 
     def own_head(e, carry):
@@ -119,13 +137,15 @@
     pl.semaphore_wait(barrier, (NZ - 1) + (NYL - 1) + 4)
 
     y_in = [
-        rcopy(rt_ref, rt2.at[:, pl.ds(TOK, TOK)], ps.at[YP_ROUTES], pr.at[YP_ROUTES], mirror),
-        rcopy(gt_ref, gt2.at[:, pl.ds(TOK, TOK)], ps.at[YP_GATES], pr.at[YP_GATES], mirror),
-        rcopy(tok_ref, tok2.at[pl.ds(TOK, TOK), :], ps.at[YP_TOK], pr.at[YP_TOK], mirror),
-        rcopy(cot_ref, cot2.at[pl.ds(TOK, TOK), :], ps.at[YP_COT], pr.at[YP_COT], mirror),
+        rcopy(rt2.at[:, own], rt2.at[:, pl.ds(TOK, TOK)], ps.at[YP_ROUTES], pr.at[YP_ROUTES], mirror),
+        rcopy(gt2.at[:, own], gt2.at[:, pl.ds(TOK, TOK)], ps.at[YP_GATES], pr.at[YP_GATES], mirror),
+        rcopy(tok2.at[own, :], tok2.at[pl.ds(TOK, TOK), :], ps.at[YP_TOK], pr.at[YP_TOK], mirror),
+        rcopy(cot2.at[own, :], cot2.at[pl.ds(TOK, TOK), :], ps.at[YP_COT], pr.at[YP_COT], mirror),
     ]
-    for cp in y_in:
+    for cp in y_in[:3]:
         cp.start()
+    local[3].wait()
+    y_in[3].start()
 
     def z_copy(src, dst, lo, size, cols, phase, other, sender):
         s_at = pl.multiple_of(other * SLOTS + lo, 16)
@@ -163,16 +183,24 @@
     rows_own, scal_own = rows.at[c], scal.at[c]
     z_send(send_tok, rows_own, 0, HEAD, full, PH_TOK_HEAD)
 
-    w_other = pl.ds(pl.multiple_of((1 - c) * HALF, 128), HALF)
-    w_mine = pl.ds(pl.multiple_of(c * HALF, 128), HALF)
     w_cp = [
-        rcopy(win_ref.at[:, w_other], wi.at[c], ss.at[SB_WIN], sr.at[SB_WIN], sib),
-        rcopy(wout_ref.at[:, w_other], wo.at[c], ss.at[SB_WOUT], sr.at[SB_WOUT], sib),
+        rcopy(win_in.at[:, w_other], wi.at[c], ss.at[SB_WIN], sr.at[SB_WIN], sib),
+        rcopy(wout_in.at[:, w_other], wo.at[c], ss.at[SB_WOUT], sr.at[SB_WOUT], sib),
     ]
     for cp in w_cp:
         cp.start()
-    wi[c] = win_ref[:, w_mine]
-    wo[c] = wout_ref[:, w_mine]
+
+    def scaled_head(e, carry):
+        choose = jnp.where(rankm[e, :, 0:TOK] == head_slot, 1.0, 0.0)
+        gate = jnp.sum(choose * gatem[e, :, 0:TOK], axis=1, keepdims=True)
+        at = pl.multiple_of(e * SLOTS, 16)
+        send_sc[pl.ds(at, HEAD), :] = (
+            gate * dot(choose.astype(BF16), cot2[0:TOK, :], NN)
+        ).astype(BF16)
+        return carry
+
+    lax.fori_loop(0, NZ, scaled_head, 0)
+    z_send(send_sc, scal_own, 0, HEAD, full, PH_SC_HEAD)
 
     r_id = lax.broadcasted_iota(jnp.int32, (SLOTS, 2 * TOK), 0)
     t_id = lax.broadcasted_iota(jnp.int32, (SLOTS, 2 * TOK), 1)
@@ -208,14 +236,14 @@
     y_in[3].wait_recv()
 
     def gather_cot(e, carry):
-        at = pl.ds(pl.multiple_of(e * SLOTS, 16), SLOTS)
+        at = pl.ds(pl.multiple_of(e * SLOTS + HEAD, 16), SLOTS - HEAD)
         choose = sel[at, :]
         gate = jnp.sum(choose * gatem[e], axis=1, keepdims=True)
         send_sc[at, :] = (gate * dot(choose.astype(BF16), cot2[...], NN)).astype(BF16)
         return carry
 
     lax.fori_loop(0, NZ, gather_cot, 0)
-    z_send(send_sc, scal_own, 0, SLOTS, full, PH_SCALED)
+    z_send(send_sc, scal_own, HEAD, SLOTS - HEAD, full, PH_SC_REST)
     scal[c, here, :] = send_sc[here, :]
 
     def gates_of(e, carry):
@@ -237,11 +265,39 @@
 
     lax.fori_loop(0, ROWS // 128, turn, 0)
 
+    def hand(buf, which, other):
+        at = pl.ds(pl.multiple_of(other * SLOTS, 16), SLOTS)
+        return rcopy(
+            buf.at[c, at, :], buf.at[c, at, :], hs.at[which, other], hr.at[which, other], sib
+        )
+
+    def take(src, dst, buf, which, phase):
+        def one(step, carry):
+            other = (z + step) % NZ
+            z_copy(src, dst, HEAD, SLOTS - HEAD, full, phase, other, other).wait_recv()
+            hand(buf, which, other).start()
+            return carry
+
+        hand(buf, which, z).start()
+        lax.fori_loop(1, NZ, one, 0)
+
+        def ready(other, carry):
+            hand(buf, which, other).wait_recv()
+            return carry
+
+        lax.fori_loop(0, NZ, ready, 0)
+
+    def handed(buf, which):
+        def one(other, carry):
+            hand(buf, which, other).wait_send()
+            return carry
+
+        lax.fori_loop(0, NZ, one, 0)
+
     z_recv(send_tok, rows_own, 0, HEAD, full, PH_TOK_HEAD)
-    z_recv(send_tok, rows_own, HEAD, SLOTS - HEAD, full, PH_TOK_REST)
-    cp_rows = rcopy(rows.at[c], rows.at[c], ss.at[SB_ROWS], sr.at[SB_ROWS], sib)
-    cp_rows.start()
-    cp_rows.wait_recv()
+    take(send_tok, rows_own, rows, 0, PH_TOK_REST)
+    for cp in local[4:]:
+        cp.wait()
 
     TILE = 320
 
@@ -274,10 +330,97 @@
     z_send(out, rout, 0, SLOTS, full, PH_OUT)
     rout[here, :] = out[here, :]
 
-    z_recv(send_sc, scal_own, 0, SLOTS, full, PH_SCALED)
-    cp_sc = rcopy(scal.at[c], scal.at[c], ss.at[SB_SCALED], sr.at[SB_SCALED], sib)
-    cp_sc.start()
-    cp_sc.wait_recv()
+    def flip(src, dst):
+        def one(i, carry):
+            at = pl.ds(pl.multiple_of(i * 128, 128), 128)
+            dst[:, at] = src[c, at, :].astype(F32).T.astype(BF16)
+            return carry
+
+        lax.fori_loop(0, ROWS // 128, one, 0)
+
+    flip(hid, hid_t)
+
+    z_recv(send_sc, scal_own, 0, HEAD, full, PH_SC_HEAD)
+    take(send_sc, scal_own, scal, 1, PH_SC_REST)
+    XW = 512
+    XH = XW // 2
+    up, dn, far = (x + 1) % NX, (x + NX - 1) % NX, (x + 2) % NX
+
+    def weigh(which, lhs, rhs):
+        for h in range(2):
+            def one(n, carry, h=h):
+                src = pl.ds(pl.multiple_of(n * 256, 256), 256)
+                dst = pl.ds(pl.multiple_of(h * HALF + n * 256, 256), 256)
+                part[which, :, dst] = dot(lhs[...], rhs[h, :, src], NN).astype(BF16)
+                return carry
+
+            lax.fori_loop(0, HALF // 256, one, 0)
+
+    def x_cols(other, half):
+        return pl.ds(pl.multiple_of(other * XW + half * XH, 256), XH)
+
+    def x_cp(which, i, src, dst, dev):
+        return rcopy(src, dst.at[which], xsm.at[which, i], xrm.at[which, i], dev)
+
+    def x_copies(which):
+        mine = part.at[which]
+        return (
+            x_cp(which, 0, mine.at[:, x_cols(far, 0)], xa, x_up),
+            x_cp(which, 1, mine.at[:, x_cols(far, 1)], xb, x_dn),
+            x_cp(which, 2, mine.at[:, x_cols(up, 1)], xd1, x_up),
+            x_cp(which, 3, mine.at[:, x_cols(dn, 0)], xd2, x_dn),
+            x_cp(which, 4, xs.at[which, 0], x1, x_up),
+            x_cp(which, 5, xs.at[which, 1], x2, x_dn),
+        )
+
+    def x_add(which, cps):
+        cps[0].wait_recv()
+        xs[which, 0] = (
+            part[which, :, x_cols(up, 0)].astype(F32) + xa[which].astype(F32)
+        ).astype(BF16)
+        cps[1].wait_recv()
+        xs[which, 1] = (
+            part[which, :, x_cols(dn, 1)].astype(F32) + xb[which].astype(F32)
+        ).astype(BF16)
+        cps[4].start()
+        cps[5].start()
+
+    def y_cols(other):
+        return pl.ds(pl.multiple_of(other * 128, 128), 128)
+
+    def y_copy(which, other, sender):
+        return rcopy(
+            xqb.at[which, :, y_cols(other)], yr.at[which, sender],
+            ys.at[which, other], yrm.at[which, sender], y_dev(other),
+        )
+
+    def y_start(which, cps):
+        for i in (2, 3, 4, 5):
+            cps[i].wait_recv()
+        mine = part.at[which]
+        xq[which, :, 0:XH] = (
+            mine[:, x_cols(x, 0)].astype(F32) + x1[which].astype(F32) + xd2[which].astype(F32)
+        )
+        xq[which, :, XH:] = (
+            mine[:, x_cols(x, 1)].astype(F32) + x2[which].astype(F32) + xd1[which].astype(F32)
+        )
+        xqb[which] = xq[which].astype(BF16)
+        for step in range(1, NYL):
+            y_copy(which, (yl + step) % NYL, yl).start()
+
+    def y_finish(which, ref):
+        total = xq[which, :, y_cols(yl)]
+        for step in range(1, NYL):
+            other = (yl + step) % NYL
+            y_copy(which, other, other).wait_recv()
+            total = total + yr[which, other].astype(F32)
+        ref[...] = total
+
+    IN, OUT = 0, 1
+    weigh(OUT, hid_t, scal)
+    x_out = x_copies(OUT)
+    for cp in x_out[:4]:
+        cp.start()
 
     def backward(i, carry):
         at = tile(i)
@@ -290,6 +433,11 @@
     lax.fori_loop(0, ROWS // TILE, backward, 0)
     cp_pre = rcopy(pre.at[c], pre.at[c], ss.at[SB_PRE], sr.at[SB_PRE], sib)
     cp_pre.start()
+    flip(pre, pre_t)
+    weigh(IN, pre_t, rows)
+    x_in = x_copies(IN)
+    x_in[0].start()
+    x_in[1].start()
     cp_pre.wait_recv()
 
     def project_back(i, carry):
@@ -298,57 +446,18 @@
         return carry
 
     lax.fori_loop(0, ROWS // TILE, project_back, 0)
-    WIDE = HALF // CHUNKS
 
     def piece(q):
-        return pl.ds(q * WIDE, WIDE)
+        return pl.ds(*PIECES[q])
 
     for q in range(CHUNKS):
         z_send(back, rback, 0, SLOTS, piece(q), PH_BACK + q)
     rback[here, :] = back[here, :]
-
-    def flip(i, carry):
-        at = pl.ds(pl.multiple_of(i * 128, 128), 128)
-        hid_t[:, at] = hid[c, at, :].astype(F32).T.astype(BF16)
-        pre_t[:, at] = pre[c, at, :].astype(F32).T.astype(BF16)
-        return carry
-
-    lax.fori_loop(0, ROWS // 128, flip, 0)
-    for h in range(2):
-        def weigh(n, carry, h=h):
-            src = pl.ds(pl.multiple_of(n * 256, 256), 256)
-            dst = pl.ds(pl.multiple_of(h * HALF + n * 256, 256), 256)
-            part[0:HID, dst] = dot(pre_t[...], rows[h, :, src], NN).astype(BF16)
-            part[HID:, dst] = dot(hid_t[...], scal[h, :, src], NN).astype(BF16)
-            return carry
-
-        lax.fori_loop(0, HALF // 256, weigh, 0)
-
-    XW = 512
-    XH = XW // 2
-
-    def x_cols(other, half):
-        return pl.ds(pl.multiple_of(other * XW + half * XH, 256), XH)
-
-    up, dn, far = (x + 1) % NX, (x + NX - 1) % NX, (x + 2) % NX
-    x_first = [
-        rcopy(part.at[:, x_cols(far, 0)], xa, xsm.at[0], xrm.at[0], x_up),
-        rcopy(part.at[:, x_cols(far, 1)], xb, xsm.at[1], xrm.at[1], x_dn),
-        rcopy(part.at[:, x_cols(up, 1)], xd1, xsm.at[2], xrm.at[2], x_up),
-        rcopy(part.at[:, x_cols(dn, 0)], xd2, xsm.at[3], xrm.at[3], x_dn),
-    ]
-    for cp in x_first:
-        cp.start()
-    x_first[0].wait_recv()
-    xs[0] = (part[:, x_cols(up, 0)].astype(F32) + xa[...].astype(F32)).astype(BF16)
-    x_first[1].wait_recv()
-    xs[1] = (part[:, x_cols(dn, 1)].astype(F32) + xb[...].astype(F32)).astype(BF16)
-    x_second = [
-        rcopy(xs.at[0], x1, xsm.at[4], xrm.at[4], x_up),
-        rcopy(xs.at[1], x2, xsm.at[5], xrm.at[5], x_dn),
-    ]
-    for cp in x_second:
-        cp.start()
+    x_add(OUT, x_out)
+    x_in[2].start()
+    x_in[3].start()
+    x_add(IN, x_in)
+    y_start(OUT, x_out)
 
     z_recv(out, rout, 0, SLOTS, full, PH_OUT)
 
@@ -376,26 +485,7 @@
     cp_gg = rcopy(ggs, ggr, ps.at[YP_GG], pr.at[YP_GG], mirror)
     cp_gg.start()
 
-    x_first[2].wait_recv()
-    x_first[3].wait_recv()
-    x_second[0].wait_recv()
-    x_second[1].wait_recv()
-    xq[:, 0:XH] = (
-        part[:, x_cols(x, 0)].astype(F32) + x1[...].astype(F32) + xd2[...].astype(F32)
-    )
-    xq[:, XH:] = (
-        part[:, x_cols(x, 1)].astype(F32) + x2[...].astype(F32) + xd1[...].astype(F32)
-    )
-    xqb[...] = xq[...].astype(BF16)
-
-    def y_cols(other):
-        return pl.ds(pl.multiple_of(other * 128, 128), 128)
-
-    def y_copy(other, sender):
-        return rcopy(xqb.at[:, y_cols(other)], yr.at[sender], ys.at[other], yrm.at[sender], y_dev(other))
-
-    for step in range(1, NYL):
-        y_copy((yl + step) % NYL, yl).start()
+    y_start(IN, x_in)
 
     cp_gg.wait_recv()
     ggm[...] = ggp[...] + ggr[...]
@@ -405,14 +495,8 @@
     mix_ref[...] = (mixo[...] + mixr[...].astype(F32)).astype(BF16)
     cp_gs.wait_recv()
     gg_ref[...] = ggm[...] + ggx[...]
-
-    total = xq[:, y_cols(yl)]
-    for step in range(1, NYL):
-        other = (yl + step) % NYL
-        y_copy(other, other).wait_recv()
-        total = total + yr[other].astype(F32)
-    gin_ref[...] = total[0:HID]
-    gout_ref[...] = total[HID:]
+    y_finish(OUT, gout_ref)
+    y_finish(IN, gin_ref)
 
     cp_back = []
     for q in range(CHUNKS):
@@ -432,16 +516,24 @@
 
     z_sent(send_tok, rows_own, 0, HEAD, full, PH_TOK_HEAD)
     z_sent(send_tok, rows_own, HEAD, SLOTS - HEAD, full, PH_TOK_REST)
-    z_sent(send_sc, scal_own, 0, SLOTS, full, PH_SCALED)
+    z_sent(send_sc, scal_own, 0, HEAD, full, PH_SC_HEAD)
+    z_sent(send_sc, scal_own, HEAD, SLOTS - HEAD, full, PH_SC_REST)
     z_sent(out, rout, 0, SLOTS, full, PH_OUT)
     for q in range(CHUNKS):
         z_sent(back, rback, 0, SLOTS, piece(q), PH_BACK + q)
-    for step in range(1, NYL):
-        y_copy((yl + step) % NYL, yl).wait_send()
-    for cp in y_in + w_cp + x_first + x_second + cp_back:
+    handed(rows, 0)
+    handed(scal, 1)
+    for which in range(2):
+        for step in range(1, NYL):
+            y_copy(which, (yl + step) % NYL, yl).wait_send()
+    for cp in (*y_in, *w_cp, *x_out, *x_in, *cp_back, cp_hid, cp_pre, cp_mix, cp_gg, cp_gs):
         cp.wait_send()
-    for cp in (cp_rows, cp_hid, cp_sc, cp_pre, cp_mix, cp_gg, cp_gs):
-        cp.wait_send()
+
+
+def write(*refs):
+    n = len(refs) // 2
+    for src, dst in zip(refs[:n], refs[n:]):
+        dst[...] = src[...]
 
 
 def per_device(tokens, routes, gates, w_in, w_out, cotangent):
@@ -457,11 +549,12 @@
             jax.ShapeDtypeStruct((HID, 128), F32),
             jax.ShapeDtypeStruct((HID, 128), F32),
         ),
-        in_specs=[vmem] * 6,
+        in_specs=[pl.BlockSpec(memory_space=pl.ANY)] * 6,
         out_specs=(vmem,) * 5,
         scratch_shapes=[
             V((2 * TOK, HALF), BF16), V((2 * TOK, HALF), BF16),
             V((4, 2 * TOK), jnp.int32), V((4, 2 * TOK), F32),
+            V((HID, 2 * HALF), BF16), V((HID, 2 * HALF), BF16),
             V((ROWS, 2 * TOK), F32), V((NZ, 1, 2 * TOK), F32), V((NZ, 1, 2 * TOK), F32),
             V((ROWS, HALF), BF16), V((ROWS, HALF), BF16),
             V((2, ROWS, HALF), BF16), V((2, ROWS, HALF), BF16),
@@ -475,21 +568,27 @@
             V((TOK, HALF), F32), V((TOK, HALF), BF16), V((TOK, HALF), BF16),
             V((4, TOK), F32), V((4, TOK), F32), V((4, TOK), F32),
             V((4, TOK), F32), V((4, TOK), F32),
-            V((2 * HID, 2 * HALF), BF16),
-            V((2 * HID, 256), BF16), V((2 * HID, 256), BF16), V((2, 2 * HID, 256), BF16),
-            V((2 * HID, 256), BF16), V((2 * HID, 256), BF16),
-            V((2 * HID, 256), BF16), V((2 * HID, 256), BF16),
-            V((2 * HID, 512), F32), V((2 * HID, 512), BF16),
-            V((NYL, 2 * HID, 128), BF16),
-            dma((PHASES, NZ)), dma((PHASES, NZ)), dma((7,)), dma((7,)),
+            V((2, HID, 2 * HALF), BF16),
+            V((2, HID, 256), BF16), V((2, HID, 256), BF16), V((2, 2, HID, 256), BF16),
+            V((2, HID, 256), BF16), V((2, HID, 256), BF16),
+            V((2, HID, 256), BF16), V((2, HID, 256), BF16),
+            V((2, HID, 512), F32), V((2, HID, 512), BF16),
+            V((2, NYL, HID, 128), BF16),
+            dma((PHASES, NZ)), dma((PHASES, NZ)), dma((5,)), dma((5,)),
+            dma((2, NZ)), dma((2, NZ)),
             dma((YP_BACK + CHUNKS,)), dma((YP_BACK + CHUNKS,)),
-            dma((6,)), dma((6,)), dma((NYL,)), dma((NYL,)),
+            dma((2, 6)), dma((2, 6)), dma((2, NYL)), dma((2, NYL)), dma((8,)),
         ],
         compiler_params=pltpu.CompilerParams(
             collective_id=0, has_side_effects=True, vmem_limit_bytes=60 * 1024 * 1024
         ),
     )(tokens, cotangent, routes.T, gates.T, w_in[0], w_out[0])
-    mixed, grad_tokens, grad_gates, grad_in, grad_out = outs
+    mixed, grad_tokens, grad_gates, grad_in, grad_out = pl.pallas_call(
+        write,
+        out_shape=tuple(jax.ShapeDtypeStruct(o.shape, o.dtype) for o in outs),
+        in_specs=[vmem] * 5,
+        out_specs=(vmem,) * 5,
+    )(*outs)
     return mixed, grad_tokens, grad_gates.T, grad_in[None], grad_out[None]
 
 

time: 165 us -> 142 us (0.86)
  the two profiles are of different devices: /device:TPU:104 before, /device:TPU:193 now
where the time goes in v2:
time: 142 us
  Pallas kernels  142 us (100%)
    pallas_call x1, Pallas kernels, per_device(): pl.pallas_call(kernel, out_shape=(jax.ShapeDtypeStruct((TOK, HALF), BF16)...  139 us

profile of v2, /device:TPU:193, one launch (start us, length us, event | category | flops | bytes accessed | tf_op | source)
XLA Modules:
  0.0 142.1 jit_solution(10158026619883153329)
XLA Ops:
  0.6 139.4 %shard_map.101 = (bf16[128,1024]{1,0:T(8,128)(2,1)}, bf16[128,1024]{1,0:T(8,128)(2,1)}, f32[4,128]{1,0:T(4,128)}, f32[384,128]{1,0:T(8,128)}, f32[384,128]{1,0:T(8,128)}) custom-call(bf16[128,1024]{1,0:T(8,128)(2,1)} %tok_in.1, bf16[128,1024]{1,0:T(8,128)(2,1)} %cot_in.1, s32[4,128]{1,0:T(4,128)} %bitcast.9, f32[4,128]{1,0:T(4,128)} %bitcast.10, ...), custom_call_target="tpu_custom_call" | custom-call | tf_op jit(solution)/shard_map/pallas_call | solution.py:543
  140.0 2.1 %shard_map.102 = (bf16[128,1024]{1,0:T(8,128)(2,1)}, bf16[128,1024]{1,0:T(8,128)(2,1)}, f32[4,128]{1,0:T(4,128)}, f32[384,128]{1,0:T(8,128)}, f32[384,128]{1,0:T(8,128)}) custom-call(bf16[128,1024]{1,0:T(8,128)(2,1)} %get-tuple-element.15.refs_0_, bf16[128,1024]{1,0:T(8,128)(2,1)} %get-tuple-element.16.refs_1_, f32[4,128]{1,0:T(4,128)} %get-tuple-element.17.refs_2_, ...), custom_call_target="tpu_custom_call" | custom-call | tf_op jit(solution)/shard_map/pallas_call | solution.py:586
